TPU v7x, 32 devices: a whole 2x2x4 slice. The times are simulated.
32 devices in a mesh: rep: 16 (over z, x, core), shard: 2 (over y).
Axes of the slice: x: 2, y: 2, z: 4, core: 2. Of those that a mesh axis runs over, the one named last changes fastest.
Arguments:
- patches: bfloat16 [16384, 1280], P(('rep', 'shard')), may hold values from -6 to 6
- lengths: int32 [32, 4], P(('rep', 'shard')), may hold values from 1 to 256, 512 in all within a row
- positions: int32 [2, 16384], P(None, ('rep', 'shard')), may hold values from 0 to 63
- ln1_gain: bfloat16 [1280], P('shard'), may hold values from 0.5 to 1.5
- ln1_bias: bfloat16 [1280], P('shard'), may hold values from -3 to 3
- qkv_weight: bfloat16 [1280, 3840], P('shard'), may hold values from -0.15625 to 0.15625
- qkv_bias: bfloat16 [3840], P('shard'), may hold values from -3 to 3
- proj_weight: bfloat16 [1280, 1280], P('shard'), may hold values from -1.25 to 1.25
- proj_bias: bfloat16 [1280], P('shard'), may hold values from -3 to 3
- ln2_gain: bfloat16 [1280], P('shard'), may hold values from 0.5 to 1.5
- ln2_bias: bfloat16 [1280], P('shard'), may hold values from -3 to 3
- fc1_weight: bfloat16 [1280, 5120], P('shard'), may hold values from -0.15625 to 0.15625
- fc1_bias: bfloat16 [5120], P('shard'), may hold values from -3 to 3
- fc2_weight: bfloat16 [5120, 1280], P('shard'), may hold values from -0.125 to 0.125
- fc2_bias: bfloat16 [1280], P('shard'), may hold values from -3 to 3
- cotangent: bfloat16 [16384, 1280], P(('rep', 'shard')), may hold values from -6 to 6
Outputs:
- layer_out: bfloat16 [16384, 1280], P(('rep', 'shard'))
- d_patches: float32 [16384, 1280], P(('rep', 'shard'))
- d_ln1_gain: float32 [1280], P('shard')
- d_ln1_bias: float32 [1280], P('shard')
- d_qkv_weight: float32 [1280, 3840], P('shard')
- d_qkv_bias: float32 [3840], P('shard')
- d_proj_weight: float32 [1280, 1280], P('shard')
- d_proj_bias: float32 [1280], P('shard')
- d_ln2_gain: float32 [1280], P('shard')
- d_ln2_bias: float32 [1280], P('shard')
- d_fc1_weight: float32 [1280, 5120], P('shard')
- d_fc1_bias: float32 [5120], P('shard')
- d_fc2_weight: float32 [5120, 1280], P('shard')
- d_fc2_bias: float32 [1280], P('shard')
Inputs may be any that keep to these rules, and one draw needn't show every extreme that they name: `lengths`: each row's entries sum to 512; its largest entry is 256.
All inputs are finite; a program needn't handle non-finite values.
Results may differ from a plain program's by a relative error of at most 0.012.
The roundings to bfloat16 on the way count: a program that leaves them out, or rounds other values in their place, can miss the bound.
Values may be sent and summed in bfloat16 or wider, within the bound.
A program may use at most 320 MiB of HBM per device.

v0:
```python
from functools import partial
import jax
import jax.numpy as jnp
from jax import lax
from jax.sharding import PartitionSpec as P

HEADS = 16
norm_eps = 1e-06
quick_slope = 1.702


def apply_layer_norm(matrix):
    center = matrix - jnp.mean(matrix, axis=-1, keepdims=True)
    spread = jnp.mean(center * center, axis=-1, keepdims=True)
    inverse_spread = lax.rsqrt(spread + norm_eps)
    return (center * inverse_spread, inverse_spread)


def norm_gradient_step(normalized_gradient, centered_standard, inverse_spread, norm_gain):
    scaled_rows = normalized_gradient * norm_gain
    return inverse_spread * (
        scaled_rows
        - jnp.mean(scaled_rows, axis=-1, keepdims=True)
        - centered_standard * jnp.mean(scaled_rows * centered_standard, axis=-1, keepdims=True)
    )


def rotary_tables(positions, head_size):
    quarter = head_size // 4
    counter = jnp.arange(quarter, dtype=jnp.float32)
    inverse = jnp.power(jnp.float32(10000.0), -2.0 * counter / (head_size // 2))
    row_angle = positions[0].astype(jnp.float32)[:, None] * inverse[None, :]
    col_angle = positions[1].astype(jnp.float32)[:, None] * inverse[None, :]
    angle = jnp.concatenate([row_angle, col_angle], axis=1)
    angle = jnp.concatenate([angle, angle], axis=1)
    return (jnp.cos(angle), jnp.sin(angle))


def apply_rotary(matrix, cosine, sine):
    half_size = matrix.shape[-1] // 2
    turned = jnp.concatenate([-matrix[..., half_size:], matrix[..., :half_size]], axis=-1)
    return matrix * cosine[:, None, :] + turned * sine[:, None, :]


def rotary_back(grad_rows, cosine, sine):
    half_size = grad_rows.shape[-1] // 2
    sined = grad_rows * sine[:, None, :]
    turned = jnp.concatenate([sined[..., half_size:], -sined[..., :half_size]], axis=-1)
    return grad_rows * cosine[:, None, :] + turned


def masked_scores(queries, keys_rot, ident, score_scale):
    scores = (
        jnp.einsum("qhd,khd->hqk", queries, keys_rot, preferred_element_type=jnp.float32)
        * score_scale
    )
    same_pic = ident[:, None] == ident[None, :]
    return jnp.where(same_pic[None], scores, -1000000000.0)


def attend(pieces, score_scale):
    queries, keys_rot, values_all, ident = pieces
    scores = masked_scores(queries, keys_rot, ident, score_scale)
    top_score = jnp.max(scores, axis=2, keepdims=True)
    exp_scores = jnp.exp(scores - top_score)
    total = jnp.sum(exp_scores, axis=2, keepdims=True)
    probs = (exp_scores / total).astype(jnp.bfloat16)
    attended = jnp.einsum("hqk,khd->qhd", probs, values_all, preferred_element_type=jnp.float32)
    return (attended, (top_score + jnp.log(total))[:, :, 0])


def attend_back(pieces, score_scale):
    queries, keys_rot, values_all, ident, grad_heads, log_total = pieces
    scores = masked_scores(queries, keys_rot, ident, score_scale)
    probs = jnp.exp(scores - log_total[:, :, None])
    grad_probs = jnp.einsum(
        "qhd,khd->hqk", grad_heads, values_all, preferred_element_type=jnp.float32
    )
    inner = jnp.sum(probs * grad_probs, axis=2, keepdims=True)
    grad_scores = (probs * (grad_probs - inner)).astype(jnp.bfloat16)
    grad_query = (
        jnp.einsum("hqk,khd->qhd", grad_scores, keys_rot, preferred_element_type=jnp.float32)
        * score_scale
    )
    grad_key = (
        jnp.einsum("hqk,qhd->khd", grad_scores, queries, preferred_element_type=jnp.float32)
        * score_scale
    )
    grad_value = jnp.einsum(
        "hqk,qhd->khd", probs.astype(jnp.bfloat16), grad_heads, preferred_element_type=jnp.float32
    )
    return (grad_query, grad_key, grad_value)


def row_product(left, right):
    return jnp.einsum("ti,tj->ij", left, right, preferred_element_type=jnp.float32)


def back_product(grad_rows, weight_full):
    return jnp.einsum("tj,ij->ti", grad_rows, weight_full, preferred_element_type=jnp.float32)


def per_device(
    patches,
    lengths,
    positions,
    ln1_gain,
    ln1_bias,
    qkv_weight,
    qkv_bias,
    proj_weight,
    proj_bias,
    ln2_gain,
    ln2_bias,
    fc1_weight,
    fc1_bias,
    fc2_weight,
    fc2_bias,
    cotangent,
):
    pack_count = lengths.shape[0]
    row_count = patches.shape[0]
    length = row_count // pack_count
    model_width = patches.shape[1]
    head_count = HEADS
    head_size = model_width // head_count
    score_scale = head_size ** (-0.5)
    pic_ends = jnp.cumsum(lengths[:, :-1], axis=1)
    slot_index = jnp.arange(length, dtype=jnp.int32)
    idents = jnp.sum((slot_index[None, :, None] >= pic_ends[:, None, :]).astype(jnp.int32), axis=2)
    cosine, sine = rotary_tables(positions, head_size)
    pack_shape = (pack_count, length, head_count, head_size)
    first_norm_gain, first_norm_bias, w_qkv, b_qkv, w_proj, b_proj = (
        lax.all_gather(ln1_gain, "shard", axis=0, tiled=True),
        lax.all_gather(ln1_bias, "shard", axis=0, tiled=True),
        lax.all_gather(qkv_weight, "shard", axis=0, tiled=True),
        lax.all_gather(qkv_bias, "shard", axis=0, tiled=True),
        lax.all_gather(proj_weight, "shard", axis=0, tiled=True),
        lax.all_gather(proj_bias, "shard", axis=0, tiled=True),
    )
    input_rows = patches.astype(jnp.float32)
    first_centered_standard, first_inverse_spread = apply_layer_norm(input_rows)
    first_normalized = (
        first_centered_standard * first_norm_gain.astype(jnp.float32)
        + first_norm_bias.astype(jnp.float32)
    ).astype(jnp.bfloat16)
    qkv_rows = jnp.dot(first_normalized, w_qkv, preferred_element_type=jnp.float32) + b_qkv.astype(
        jnp.float32
    )
    qkv_rows = qkv_rows.reshape(row_count, 3, head_count, head_size)
    queries = apply_rotary(qkv_rows[:, 0], cosine, sine).astype(jnp.bfloat16).reshape(pack_shape)
    keys_rot = apply_rotary(qkv_rows[:, 1], cosine, sine).astype(jnp.bfloat16).reshape(pack_shape)
    values_all = qkv_rows[:, 2].astype(jnp.bfloat16).reshape(pack_shape)
    attended, log_total = lax.map(
        partial(attend, score_scale=score_scale), (queries, keys_rot, values_all, idents)
    )
    heads_out = attended.reshape(row_count, model_width).astype(jnp.bfloat16)
    hidden_rows = (
        input_rows
        + jnp.dot(heads_out, w_proj, preferred_element_type=jnp.float32)
        + b_proj.astype(jnp.float32)
    )
    second_norm_gain, second_norm_bias, w_up, b_up, w_down, b_down = (
        lax.all_gather(ln2_gain, "shard", axis=0, tiled=True),
        lax.all_gather(ln2_bias, "shard", axis=0, tiled=True),
        lax.all_gather(fc1_weight, "shard", axis=0, tiled=True),
        lax.all_gather(fc1_bias, "shard", axis=0, tiled=True),
        lax.all_gather(fc2_weight, "shard", axis=0, tiled=True),
        lax.all_gather(fc2_bias, "shard", axis=0, tiled=True),
    )
    second_centered_standard, second_inverse_spread = apply_layer_norm(hidden_rows)
    second_normalized = (
        second_centered_standard * second_norm_gain.astype(jnp.float32)
        + second_norm_bias.astype(jnp.float32)
    ).astype(jnp.bfloat16)
    up_pre = jnp.dot(second_normalized, w_up, preferred_element_type=jnp.float32) + b_up.astype(
        jnp.float32
    )
    sigmoid_up = 1.0 / (1.0 + jnp.exp(-quick_slope * up_pre))
    activation = (up_pre * sigmoid_up).astype(jnp.bfloat16)
    out_full = (
        hidden_rows
        + jnp.dot(activation, w_down, preferred_element_type=jnp.float32)
        + b_down.astype(jnp.float32)
    )
    layer_out = out_full.astype(jnp.bfloat16)
    second_norm_gain, second_norm_bias, w_up, b_up, w_down, b_down = (
        lax.all_gather(ln2_gain, "shard", axis=0, tiled=True),
        lax.all_gather(ln2_bias, "shard", axis=0, tiled=True),
        lax.all_gather(fc1_weight, "shard", axis=0, tiled=True),
        lax.all_gather(fc1_bias, "shard", axis=0, tiled=True),
        lax.all_gather(fc2_weight, "shard", axis=0, tiled=True),
        lax.all_gather(fc2_bias, "shard", axis=0, tiled=True),
    )
    grad_out = cotangent.astype(jnp.float32)
    d_w_down = row_product(activation, cotangent)
    d_b_down = jnp.sum(grad_out, axis=0)
    grad_act = back_product(cotangent, w_down)
    slope_up = sigmoid_up + quick_slope * up_pre * sigmoid_up * (1.0 - sigmoid_up)
    grad_pre = (grad_act * slope_up).astype(jnp.bfloat16)
    d_w_up = row_product(second_normalized, grad_pre)
    d_b_up = jnp.sum(grad_pre.astype(jnp.float32), axis=0)
    second_normalized_gradient = back_product(grad_pre, w_up)
    second_gain_gradient = jnp.sum(second_normalized_gradient * second_centered_standard, axis=0)
    d_bias_two = jnp.sum(second_normalized_gradient, axis=0)
    grad_hidden = grad_out + norm_gradient_step(
        second_normalized_gradient,
        second_centered_standard,
        second_inverse_spread,
        second_norm_gain.astype(jnp.float32),
    )
    m_gain, m_bias, m_up, m_upb, m_down, m_downb = (
        lax.psum_scatter(second_gain_gradient, "shard", scatter_dimension=0, tiled=True),
        lax.psum_scatter(d_bias_two, "shard", scatter_dimension=0, tiled=True),
        lax.psum_scatter(d_w_up, "shard", scatter_dimension=0, tiled=True),
        lax.psum_scatter(d_b_up, "shard", scatter_dimension=0, tiled=True),
        lax.psum_scatter(d_w_down, "shard", scatter_dimension=0, tiled=True),
        lax.psum_scatter(d_b_down, "shard", scatter_dimension=0, tiled=True),
    )
    m_gain, m_bias, m_up, m_upb, m_down, m_downb = lax.psum(
        (m_gain, m_bias, m_up, m_upb, m_down, m_downb), "rep"
    )
    first_norm_gain, first_norm_bias, w_qkv, b_qkv, w_proj, b_proj = (
        lax.all_gather(ln1_gain, "shard", axis=0, tiled=True),
        lax.all_gather(ln1_bias, "shard", axis=0, tiled=True),
        lax.all_gather(qkv_weight, "shard", axis=0, tiled=True),
        lax.all_gather(qkv_bias, "shard", axis=0, tiled=True),
        lax.all_gather(proj_weight, "shard", axis=0, tiled=True),
        lax.all_gather(proj_bias, "shard", axis=0, tiled=True),
    )
    grad_branch = grad_hidden.astype(jnp.bfloat16)
    d_w_proj = row_product(heads_out, grad_branch)
    d_b_proj = jnp.sum(grad_branch.astype(jnp.float32), axis=0)
    grad_heads = back_product(grad_branch, w_proj).astype(jnp.bfloat16).reshape(pack_shape)
    grad_query, grad_key, grad_value = lax.map(
        partial(attend_back, score_scale=score_scale),
        (queries, keys_rot, values_all, idents, grad_heads, log_total),
    )
    rows_shape = (row_count, head_count, head_size)
    grad_query = rotary_back(grad_query.reshape(rows_shape), cosine, sine)
    grad_key = rotary_back(grad_key.reshape(rows_shape), cosine, sine)
    grad_qkv = (
        jnp.stack([grad_query, grad_key, grad_value.reshape(rows_shape)], axis=1)
        .reshape(row_count, 3 * model_width)
        .astype(jnp.bfloat16)
    )
    d_w_qkv = row_product(first_normalized, grad_qkv)
    d_b_qkv = jnp.sum(grad_qkv.astype(jnp.float32), axis=0)
    first_normalized_gradient = back_product(grad_qkv, w_qkv)
    first_gain_gradient = jnp.sum(first_normalized_gradient * first_centered_standard, axis=0)
    d_bias_one = jnp.sum(first_normalized_gradient, axis=0)
    d_patches = grad_hidden + norm_gradient_step(
        first_normalized_gradient,
        first_centered_standard,
        first_inverse_spread,
        first_norm_gain.astype(jnp.float32),
    )
    a_gain, a_bias, a_qkv, a_qkvb, a_proj, a_projb = (
        lax.psum_scatter(first_gain_gradient, "shard", scatter_dimension=0, tiled=True),
        lax.psum_scatter(d_bias_one, "shard", scatter_dimension=0, tiled=True),
        lax.psum_scatter(d_w_qkv, "shard", scatter_dimension=0, tiled=True),
        lax.psum_scatter(d_b_qkv, "shard", scatter_dimension=0, tiled=True),
        lax.psum_scatter(d_w_proj, "shard", scatter_dimension=0, tiled=True),
        lax.psum_scatter(d_b_proj, "shard", scatter_dimension=0, tiled=True),
    )
    a_gain, a_bias, a_qkv, a_qkvb, a_proj, a_projb = lax.psum(
        (a_gain, a_bias, a_qkv, a_qkvb, a_proj, a_projb), "rep"
    )
    return (
        layer_out,
        d_patches,
        a_gain,
        a_bias,
        a_qkv,
        a_qkvb,
        a_proj,
        a_projb,
        m_gain,
        m_bias,
        m_up,
        m_upb,
        m_down,
        m_downb,
    )


def solution(mesh):
    in_specs = (
        P(("rep", "shard"), None),
        P(("rep", "shard"), None),
        P(None, ("rep", "shard")),
        P("shard"),
        P("shard"),
        P("shard", None),
        P("shard"),
        P("shard", None),
        P("shard"),
        P("shard"),
        P("shard"),
        P("shard", None),
        P("shard"),
        P("shard", None),
        P("shard"),
        P(("rep", "shard"), None),
    )
    out_specs = (
        P(("rep", "shard"), None),
        P(("rep", "shard"), None),
        P("shard"),
        P("shard"),
        P("shard", None),
        P("shard"),
        P("shard", None),
        P("shard"),
        P("shard"),
        P("shard"),
        P("shard", None),
        P("shard"),
        P("shard", None),
        P("shard"),
    )
    return jax.shard_map(
        per_device, mesh=mesh, in_specs=in_specs, out_specs=out_specs, check_vma=False
    )
```

profile of v0, /device:TPU:0, one launch (start us, length us, event | category | flops | bytes accessed | tf_op | source)
XLA Modules:
  0.0 2157.3 jit_solution(15266474193244514854)
XLA Ops:
  45.8 89.2 %all-gather.13.cloned.1.call-done = bf16[1280,3840]{1,0:T(8,128)(2,1)} async-done(((bf16[640,3840]{1,0:T(8,128)(2,1)}), bf16[1280,3840]{1,0:T(8,128)(2,1)}) %all-gather.13.cloned.1.call-update) | async-done | bytes 9830416 | tf_op jit(solution)/shard_map/all_gather | solution.py:136
  135.0 11.5 convolution_add_fusion
  146.6 9.2 copy.51
  178.9 10.5 fusion.32
  195.7 147.2 %all-gather.17.cloned.1.call-done = bf16[1280,5120]{1,0:T(8,128)(2,1)} async-done(((bf16[640,5120]{1,0:T(8,128)(2,1)}), bf16[1280,5120]{1,0:T(8,128)(2,1)}) %all-gather.17.cloned.1.call-update) | async-done | bytes 13107216 | tf_op jit(solution)/shard_map/all_gather | solution.py:166
  342.9 13.6 fusion.47
  356.5 146.1 %all-gather.19.cloned.1.call-done = bf16[5120,1280]{1,0:T(8,128)(2,1)} async-done(((bf16[2560,1280]{1,0:T(8,128)(2,1)}), bf16[5120,1280]{1,0:T(8,128)(2,1)}) %all-gather.19.cloned.1.call-update) | async-done | bytes 13107216 | tf_op jit(solution)/shard_map/all_gather | solution.py:168
  502.6 16.9 convert_reduce_fusion
  519.4 15.0 multiply_reduce_fusion.1
  552.5 12.1 multiply_reduce_fusion
  564.6 12.1 multiply_convert_fusion
  583.9 8.7 fusion.29
  595.6 10.0 fusion.43
  605.7 15.4 fusion.48
  621.2 15.4 fusion.46
  637.3 12.7 fusion.21
  650.1 196.3 %reduce-scatter.5.cloned.1.call-done = f32[640,3840]{1,0:T(8,128)} async-done(((f32[1280,3840]{1,0:T(8,128)}), f32[640,3840]{1,0:T(8,128)}) %reduce-scatter.5.cloned.1.call-update) | async-done | bytes 9830416 | tf_op jit(solution)/shard_map/reduce_scatter | solution.py:261
  846.5 293.0 %reduce-scatter.11.cloned.1.call-done = f32[2560,1280]{1,0:T(8,128)} async-done(((f32[5120,1280]{1,0:T(8,128)}), f32[2560,1280]{1,0:T(8,128)}) %reduce-scatter.11.cloned.1.call-update) | async-done | bytes 13107216 | tf_op jit(solution)/shard_map/reduce_scatter | solution.py:217
  1139.5 293.0 %reduce-scatter.9.cloned.1.call-done = f32[640,5120]{1,0:T(8,128)} async-done(((f32[1280,5120]{1,0:T(8,128)}), f32[640,5120]{1,0:T(8,128)}) %reduce-scatter.9.cloned.1.call-update) | async-done | bytes 13107216 | tf_op jit(solution)/shard_map/reduce_scatter | solution.py:215
  1445.4 15.7 fusion.14
  1467.3 63.9 %all-reduce.8 = (f32[640]{0:T(1024)}, f32[640]{0:T(1024)}, f32[1920]{0:T(1024)}, f32[640]{0:T(1024)}, f32[640]{0:T(1024)}, /*index=5*/f32[640]{0:T(1024)}, f32[2560]{0:T(1024)}, f32[640]{0:T(1024)}) all-reduce(f32[640]{0:T(1024)S(1)} %dynamic-slice.4, f32[640]{0:T(1024)S(1)} %dynamic-slice.6, ...), channel_id=1, replica_groups=mesh['rep'=16,'shard'=2] {'rep'}, use_global_device_ids=true, to_apply=%region_15.16 | all-reduce | flops 8320 | bytes 66560 | tf_op jit(solution)/shard_map/psum | solution.py:266
  1531.3 586.7 %all-reduce.14.cloned.1.call-done = (f32[640,3840]{1,0:T(8,128)}, f32[640,1280]{1,0:T(8,128)}, f32[640,5120]{1,0:T(8,128)}, f32[2560,1280]{1,0:T(8,128)}) async-done(((f32[640,3840]{1,0:T(8,128)}, f32[640,1280]{1,0:T(8,128)}, f32[640,5120]{1,0:T(8,128)}, f32[2560,1280]{1,0:T(8,128)}), (f32[640,3840]{1,0:T(8,128)}, f32[640,1280]{1,0:T(8,128)}, f32[640,5120]{1,0:T(8,128)}, ...) | async-done | bytes 39321616 | tf_op jit(solution)/shard_map/psum | solution.py:266
  2128.2 11.3 copy.75
  2139.5 10.5 copy.76
  (173 shorter events, 123.9 us)
Async XLA Ops:
  7.2 127.8 %all-gather.13.cloned.1.call-start = ((), (), s32[]{:S(2)}) async-start(), calls=%async_computation.4 | async-start | bytes 14745600 | tf_op jit(solution)/shard_map/all_gather | solution.py:136
  7.9 181.4 %all-gather.15.cloned.1.call-start = ((), (), s32[]{:S(2)}) async-start(), calls=%async_computation.5 | async-start | bytes 4915200 | tf_op jit(solution)/shard_map/all_gather | solution.py:138
  8.7 334.2 %all-gather.17.cloned.1.call-start = ((), (), s32[]{:S(2)}) async-start(), calls=%async_computation.6 | async-start | bytes 19660800 | tf_op jit(solution)/shard_map/all_gather | solution.py:166
  9.5 24.0 %copy-start.23 = (bf16[1920]{0:T(1024)(128)(2,1)S(1)}, bf16[1920]{0:T(1024)(128)(2,1)}, u32[]{:S(2)}) copy-start(bf16[1920]{0:T(1024)(128)(2,1)} %param.22) | copy-start | bytes 11524
  9.5 28.8 %copy-start.22 = (bf16[2560]{0:T(1024)(128)(2,1)S(1)}, bf16[2560]{0:T(1024)(128)(2,1)}, u32[]{:S(2)}) copy-start(bf16[2560]{0:T(1024)(128)(2,1)} %param.28) | copy-start | bytes 15364
  9.5 33.6 %copy-start.31 = (s32[1,4]{1,0:T(1,128)S(1)}, s32[1,4]{1,0:T(1,128)}, u32[]{:S(2)}) copy-start(s32[1,4]{1,0:T(1,128)} %param.17) | copy-start | bytes 52
  9.5 33.9 %copy-start.24 = (s32[2,512]{1,0:T(2,128)S(1)}, s32[2,512]{1,0:T(2,128)}, u32[]{:S(2)}) copy-start(s32[2,512]{1,0:T(2,128)} %param.18) | copy-start | bytes 12292
  9.5 35.3 %copy-start.1 = (bf16[512,1280]{1,0:T(8,128)(2,1)S(1)}, bf16[512,1280]{1,0:T(8,128)(2,1)}, u32[]{:S(2)}) copy-start(bf16[512,1280]{1,0:T(8,128)(2,1)} %param.16) | copy-start | bytes 3932164
  9.5 493.1 %all-gather.19.cloned.1.call-start = ((), (), s32[]{:S(2)}) async-start(), calls=%async_computation.7 | async-start | bytes 19660800 | tf_op jit(solution)/shard_map/all_gather | solution.py:168
  10.1 640.1 %reduce-scatter.7.cloned.1.call-start = ((), (), s32[]{:S(2)}) async-start(), calls=%async_computation.9 | async-start | bytes 9830400 | tf_op jit(solution)/shard_map/reduce_scatter | solution.py:263
  20.0 126.6 %copy-start.14 = (f32[1280]{0:T(1024)}, f32[1280]{0:T(1024)S(1)}, u32[]{:S(2)}) copy-start(f32[1280]{0:T(1024)S(1)} %reshape.326) | copy-start | bytes 15364
  28.8 117.7 %copy-start.20 = (f32[1280]{0:T(1024)}, f32[1280]{0:T(1024)S(1)}, u32[]{:S(2)}) copy-start(f32[1280]{0:T(1024)S(1)} %reshape.327) | copy-start | bytes 15364
  45.0 101.5 %copy-start.16 = (f32[512]{0:T(512)}, f32[512]{0:T(512)S(1)}, u32[]{:S(2)}) copy-start(f32[512]{0:T(512)S(1)} %broadcast_multiply_fusion.9) | copy-start | bytes 6148
  45.5 101.0 %copy-start.18 = (f32[512]{0:T(512)}, f32[512]{0:T(512)S(1)}, u32[]{:S(2)}) copy-start(f32[512]{0:T(512)S(1)} %add_rsqrt_fusion.1) | copy-start | bytes 6148
  162.9 7.7 copy-start.3
  162.9 7.7 copy-start.6
  519.4 15.0 copy-start.11
  543.9 302.6 %reduce-scatter.5.cloned.1.call-start = ((), (), s32[]{:S(2)}) async-start(), calls=%async_computation.8 | async-start | bytes 29491200 | tf_op jit(solution)/shard_map/reduce_scatter | solution.py:261
  564.6 12.1 copy-start.7
  605.7 533.8 %reduce-scatter.11.cloned.1.call-start = ((), (), s32[]{:S(2)}) async-start(), calls=%async_computation.11 | async-start | bytes 39321600 | tf_op jit(solution)/shard_map/reduce_scatter | solution.py:217
  621.1 811.3 %reduce-scatter.9.cloned.1.call-start = ((), (), s32[]{:S(2)}) async-start(), calls=%async_computation.10 | async-start | bytes 39321600 | tf_op jit(solution)/shard_map/reduce_scatter | solution.py:215
  636.6 824.6 %all-reduce.16.cloned.1.call-start = ((), (), s32[]{:S(2)}) async-start(), calls=%async_computation.13 | async-start | bytes 172032
  650.1 1468.0 %all-reduce.14.cloned.1.call-start = ((), (), s32[]{:S(2)}) async-start(), calls=%async_computation.12 | async-start | bytes 78643200 | tf_op jit(solution)/shard_map/psum | solution.py:266
  2118.0 8.5 copy-start.10
  (21 other events, 44.9 us)
Sparse Core Ops, SparseCore 0:
  9.5 125.4 all-gather.12
  136.6 46.4 all-gather.14
  184.6 158.2 all-gather.16
  344.3 158.2 all-gather.18
  544.0 79.9 reduce-scatter.6
  626.2 220.1 reduce-scatter.4
  848.8 290.6 reduce-scatter.10
  1141.8 290.6 reduce-scatter.8
  1436.3 20.8 all-reduce.15
  1461.9 656.1 all-reduce.13
where the time goes:
time: 2170 us; the launch traced here: 2160 us
  waiting for transfers between devices  1750 us (81%)
  matrix products  186 us (9%)
  blocking collectives  101 us (5%)
  local copies, waits for them, and re-layouts  60.9 us (3%)
  other arithmetic  38 us (2%)
    psum x1, waiting for transfers between devices, per_device(): lax.psum((a_gain, a_bias, a_qkv, a_qkvb, a_proj, a_projb), 'rep')  587 us
    reduce_scatter x1, waiting for transfers between devices, per_device(): lax.psum_scatter(d_w_down, 'shard', scatter_dimension=0, tiled=True)  293 us
    reduce_scatter x1, waiting for transfers between devices, per_device(): lax.psum_scatter(d_w_up, 'shard', scatter_dimension=0, tiled=True)  293 us
    reduce_scatter x1, waiting for transfers between devices, per_device(): lax.psum_scatter(d_w_qkv, 'shard', scatter_dimension=0, tiled=True)  196 us
    all_gather x1, waiting for transfers between devices, per_device(): lax.all_gather(fc1_weight, 'shard', axis=0, tiled=True)  147 us
    all_gather x1, waiting for transfers between devices, per_device(): lax.all_gather(fc2_weight, 'shard', axis=0, tiled=True)  146 us
    all_gather x1, waiting for transfers between devices, per_device(): lax.all_gather(qkv_weight, 'shard', axis=0, tiled=True)  89.2 us
    psum x1, blocking collectives, per_device(): lax.psum((a_gain, a_bias, a_qkv, a_qkvb, a_proj, a_projb), 'rep')  63.9 us
  transfers between devices with their start and end apart: 10, of which 7 were waited for; matrix products, arithmetic and copies ran while one was open for 10% of the time, Pallas kernels for 0%

commit v1 on v0

--- a/solution.py
+++ b/solution.py
@@ -7,6 +7,18 @@
 HEADS = 16
 norm_eps = 1e-06
 quick_slope = 1.702
+
+
+def gather_by_bits(x, axis, dim):
+    ways, here, step = (lax.axis_size(axis), lax.axis_index(axis), x.shape[dim])
+    line, have = (x, 1)
+    while have < ways:
+        line = jnp.concatenate(
+            [line, lax.ppermute(line, axis, [(d, (d - have) % ways) for d in range(ways)])],
+            axis=dim,
+        )
+        have = 2 * have
+    return jnp.roll(line, here * step, axis=dim)
 
 
 def apply_layer_norm(matrix):
@@ -163,7 +175,7 @@
     second_norm_gain, second_norm_bias, w_up, b_up, w_down, b_down = (
         lax.all_gather(ln2_gain, "shard", axis=0, tiled=True),
         lax.all_gather(ln2_bias, "shard", axis=0, tiled=True),
-        lax.all_gather(fc1_weight, "shard", axis=0, tiled=True),
+        gather_by_bits(fc1_weight, "shard", 0),
         lax.all_gather(fc1_bias, "shard", axis=0, tiled=True),
         lax.all_gather(fc2_weight, "shard", axis=0, tiled=True),
         lax.all_gather(fc2_bias, "shard", axis=0, tiled=True),

time: 2170 us -> 2260 us (1.041)
  blocking collectives: 101 us -> 351 us
  waiting for transfers between devices: 1750 us -> 1590 us
    all_gather x1, blocking collectives: 4.6 us -> 255 us  [per_device(): lax.all_gather(proj_bias, 'shard', axis=0, tiled=True)]
    all_gather x1, waiting for transfers between devices: 89.2 us -> 0.01 us  [per_device(): lax.all_gather(qkv_weight, 'shard', axis=0, tiled=True)]
    all_gather x1, waiting for transfers between devices: 146 us -> 71.5 us  [per_device(): lax.all_gather(fc2_weight, 'shard', axis=0, tiled=True)]
  transfers between devices with their start and end apart: 10 -> 11, of which waited for: 7 -> 6; matrix products, arithmetic and copies ran while one was open for 10% -> 10% of each run, Pallas kernels for 0% -> 0%
where the time goes in v1:
time: 2260 us; the launch traced here: 2250 us
  waiting for transfers between devices  1590 us (70%)
  blocking collectives  351 us (16%)
  matrix products  197 us (9%)
  local copies, waits for them, and re-layouts  61.8 us (3%)
  other arithmetic  37.9 us (2%)
    psum x1, waiting for transfers between devices, per_device(): lax.psum((a_gain, a_bias, a_qkv, a_qkvb, a_proj, a_projb), 'rep')  587 us
    reduce_scatter x1, waiting for transfers between devices, per_device(): lax.psum_scatter(d_w_down, 'shard', scatter_dimension=0, tiled=True)  293 us
    reduce_scatter x1, waiting for transfers between devices, per_device(): lax.psum_scatter(d_w_up, 'shard', scatter_dimension=0, tiled=True)  293 us
    all_gather x1, blocking collectives, per_device(): lax.all_gather(proj_bias, 'shard', axis=0, tiled=True)  255 us
    reduce_scatter x1, waiting for transfers between devices, per_device(): lax.psum_scatter(d_w_qkv, 'shard', scatter_dimension=0, tiled=True)  196 us
    all_gather x1, waiting for transfers between devices, per_device(): lax.all_gather(fc1_weight, 'shard', axis=0, tiled=True)  143 us
    all_gather x1, waiting for transfers between devices, per_device(): lax.all_gather(fc2_weight, 'shard', axis=0, tiled=True)  71.5 us
    psum x1, blocking collectives, per_device(): lax.psum((a_gain, a_bias, a_qkv, a_qkvb, a_proj, a_projb), 'rep')  63.9 us
  transfers between devices with their start and end apart: 11, of which 6 were waited for; matrix products, arithmetic and copies ran while one was open for 10% of the time, Pallas kernels for 0%

profile of v1, /device:TPU:0, one launch (start us, length us, event | category | flops | bytes accessed | tf_op | source)
XLA Modules:
  0.0 2254.3 jit_solution(1124208430337465535)
XLA Ops:
  12.7 255.3 %all-gather.3 = bf16[2,1,640]{2,1,0:T(2,128)(2,1)S(1)} all-gather(bf16[1,1,640]{2,1,0:T(2,128)(2,1)S(1)} %reshape.316), channel_id=1, replica_groups=mesh['rep'=16,'shard'=2] {'shard'}, dimensions={0}, use_global_device_ids=true | all-gather | bytes 3840 | tf_op jit(solution)/shard_map/all_gather | solution.py:151
  298.7 12.1 convolution_add_fusion
  310.8 9.6 copy.51
  344.0 10.5 fusion.37
  359.7 25.3 %fusion.4 = f32[512,5120]{1,0:T(8,128)} fusion(s32[]{:T(128)S(6)} %select_n.22, bf16[640,5120]{1,0:T(8,128)(2,1)} %param.27, bf16[640,5120]{1,0:T(8,128)(2,1)} %collective-permute-done, f32[512,1280]{1,0:T(8,128)S(1)} %get-tuple-element.125, f32[1280]{0:T(1024)S(1)} %reshape.331, f32[1280]{0:T(1024)S(1)} %reshape.330, f32[512]{0:T(512)S(1)} %add_rsqrt_fusion, ...), kind=kOutput, calls=%fused_computation.14 | convolution fusion | flops 6766592000 | bytes 26228740 | tf_op jit(solution)/shard_map/dot_general | solution.py:188
  385.0 71.5 %all-gather.17.cloned.1.call-done = bf16[5120,1280]{1,0:T(8,128)(2,1)} async-done(((bf16[2560,1280]{1,0:T(8,128)(2,1)}), bf16[5120,1280]{1,0:T(8,128)(2,1)}) %all-gather.17.cloned.1.call-update) | async-done | bytes 13107216 | tf_op jit(solution)/shard_map/all_gather | solution.py:180
  456.5 16.5 convert_reduce_fusion
  472.9 143.2 %all-gather.19.cloned.1.call-done = bf16[1280,5120]{1,0:T(8,128)(2,1)} async-done(((bf16[640,5120]{1,0:T(8,128)(2,1)}), bf16[1280,5120]{1,0:T(8,128)(2,1)}) %all-gather.19.cloned.1.call-update) | async-done | bytes 13107216 | tf_op jit(solution)/shard_map/all_gather | solution.py:202
  616.2 15.3 multiply_reduce_fusion.1
  649.6 12.1 multiply_reduce_fusion
  661.7 12.1 multiply_convert_fusion
  680.9 8.7 fusion.34
  692.7 10.0 fusion.50
  702.8 15.4 fusion.54
  718.3 15.4 fusion.53
  734.4 12.7 fusion.26
  747.2 196.3 %reduce-scatter.5.cloned.1.call-done = f32[640,3840]{1,0:T(8,128)} async-done(((f32[1280,3840]{1,0:T(8,128)}), f32[640,3840]{1,0:T(8,128)}) %reduce-scatter.5.cloned.1.call-update) | async-done | bytes 9830416 | tf_op jit(solution)/shard_map/reduce_scatter | solution.py:273
  943.6 293.0 %reduce-scatter.11.cloned.1.call-done = f32[2560,1280]{1,0:T(8,128)} async-done(((f32[5120,1280]{1,0:T(8,128)}), f32[2560,1280]{1,0:T(8,128)}) %reduce-scatter.11.cloned.1.call-update) | async-done | bytes 13107216 | tf_op jit(solution)/shard_map/reduce_scatter | solution.py:229
  1236.5 293.0 %reduce-scatter.9.cloned.1.call-done = f32[640,5120]{1,0:T(8,128)} async-done(((f32[1280,5120]{1,0:T(8,128)}), f32[640,5120]{1,0:T(8,128)}) %reduce-scatter.9.cloned.1.call-update) | async-done | bytes 13107216 | tf_op jit(solution)/shard_map/reduce_scatter | solution.py:227
  1542.5 15.7 fusion.19
  1564.5 63.9 %all-reduce.8 = (f32[640]{0:T(1024)}, f32[640]{0:T(1024)}, f32[1920]{0:T(1024)}, f32[640]{0:T(1024)}, f32[640]{0:T(1024)}, /*index=5*/f32[640]{0:T(1024)}, f32[2560]{0:T(1024)}, f32[640]{0:T(1024)}) all-reduce(f32[640]{0:T(1024)S(1)} %dynamic-slice.4, f32[640]{0:T(1024)S(1)} %dynamic-slice.6, ...), channel_id=1, replica_groups=mesh['rep'=16,'shard'=2] {'rep'}, use_global_device_ids=true, to_apply=%region_15.16 | all-reduce | flops 8320 | bytes 66560 | tf_op jit(solution)/shard_map/psum | solution.py:278
  1628.4 586.7 %all-reduce.14.cloned.1.call-done = (f32[640,3840]{1,0:T(8,128)}, f32[640,1280]{1,0:T(8,128)}, f32[640,5120]{1,0:T(8,128)}, f32[2560,1280]{1,0:T(8,128)}) async-done(((f32[640,3840]{1,0:T(8,128)}, f32[640,1280]{1,0:T(8,128)}, f32[640,5120]{1,0:T(8,128)}, f32[2560,1280]{1,0:T(8,128)}), (f32[640,3840]{1,0:T(8,128)}, f32[640,1280]{1,0:T(8,128)}, f32[640,5120]{1,0:T(8,128)}, ...) | async-done | bytes 39321616 | tf_op jit(solution)/shard_map/psum | solution.py:278
  2225.3 11.3 copy.75
  2236.5 10.5 copy.76
  (175 shorter events, 120.9 us)
Async XLA Ops:
  7.2 291.6 %all-gather.13.cloned.1.call-start = ((), (), s32[]{:S(2)}) async-start(), calls=%async_computation.4 | async-start | bytes 14745600 | tf_op jit(solution)/shard_map/all_gather | solution.py:148
  7.9 346.6 %all-gather.15.cloned.1.call-start = ((), (), s32[]{:S(2)}) async-start(), calls=%async_computation.5 | async-start | bytes 4915200 | tf_op jit(solution)/shard_map/all_gather | solution.py:150
  8.7 447.8 %all-gather.17.cloned.1.call-start = ((), (), s32[]{:S(2)}) async-start(), calls=%async_computation.6 | async-start | bytes 19660800 | tf_op jit(solution)/shard_map/all_gather | solution.py:180
  9.4 258.7 %copy-start.23 = (bf16[1920]{0:T(1024)(128)(2,1)S(1)}, bf16[1920]{0:T(1024)(128)(2,1)}, u32[]{:S(2)}) copy-start(bf16[1920]{0:T(1024)(128)(2,1)} %param.22) | copy-start | bytes 11524
  9.4 263.7 %copy-start.26 = (bf16[640]{0:T(1024)(128)(2,1)S(1)}, bf16[640]{0:T(1024)(128)(2,1)}, u32[]{:S(2)}) copy-start(bf16[640]{0:T(1024)(128)(2,1)} %param.20) | copy-start | bytes 3844
  9.4 268.3 %copy-start.27 = (bf16[640]{0:T(1024)(128)(2,1)S(1)}, bf16[640]{0:T(1024)(128)(2,1)}, u32[]{:S(2)}) copy-start(bf16[640]{0:T(1024)(128)(2,1)} %param.19) | copy-start | bytes 3844
  9.4 272.9 %copy-start.1 = (bf16[512,1280]{1,0:T(8,128)(2,1)S(1)}, bf16[512,1280]{1,0:T(8,128)(2,1)}, u32[]{:S(2)}) copy-start(bf16[512,1280]{1,0:T(8,128)(2,1)} %param.16) | copy-start | bytes 3932164
  9.5 606.7 %all-gather.19.cloned.1.call-start = ((), (), s32[]{:S(2)}) async-start(), calls=%async_computation.7 | async-start | bytes 19660800 | tf_op jit(solution)/shard_map/all_gather | solution.py:202
  9.5 350.2 %collective-permute-start = (bf16[640,5120]{1,0:T(8,128)(2,1)}, bf16[640,5120]{1,0:T(8,128)(2,1)}, u32[]{:S(2)}, u32[]{:S(2)}) collective-permute-start(bf16[640,5120]{1,0:T(8,128)(2,1)} %param.27), channel_id=1, source_target_pairs={{0,1},{1,0},{2,3},{3,2},{4,5},{5,4},{6,7},{7,6},{8,9},{9,8},{10,11... | collective-permute-start | bytes 19660808 | tf_op jit(solution)/shard_map/ppermute | solution.py:17
  12.6 270.5 %copy-start.24 = (s32[2,512]{1,0:T(2,128)S(1)}, s32[2,512]{1,0:T(2,128)}, u32[]{:S(2)}) copy-start(s32[2,512]{1,0:T(2,128)} %param.18) | copy-start | bytes 12292
  12.6 270.6 %copy-start.31 = (s32[1,4]{1,0:T(1,128)S(1)}, s32[1,4]{1,0:T(1,128)}, u32[]{:S(2)}) copy-start(s32[1,4]{1,0:T(1,128)} %param.17) | copy-start | bytes 52
  12.6 271.1 %copy-start.28 = (bf16[640]{0:T(1024)(128)(2,1)S(1)}, bf16[640]{0:T(1024)(128)(2,1)}, u32[]{:S(2)}) copy-start(bf16[640]{0:T(1024)(128)(2,1)} %param.26) | copy-start | bytes 3844
  12.6 275.7 %copy-start.29 = (bf16[640]{0:T(1024)(128)(2,1)S(1)}, bf16[640]{0:T(1024)(128)(2,1)}, u32[]{:S(2)}) copy-start(bf16[640]{0:T(1024)(128)(2,1)} %param.25) | copy-start | bytes 3844
  12.6 280.3 %copy-start.22 = (bf16[2560]{0:T(1024)(128)(2,1)S(1)}, bf16[2560]{0:T(1024)(128)(2,1)}, u32[]{:S(2)}) copy-start(bf16[2560]{0:T(1024)(128)(2,1)} %param.28) | copy-start | bytes 15364
  12.6 734.6 %reduce-scatter.7.cloned.1.call-start = ((), (), s32[]{:S(2)}) async-start(), calls=%async_computation.9 | async-start | bytes 9830400 | tf_op jit(solution)/shard_map/reduce_scatter | solution.py:275
  277.7 33.1 %copy-start.20 = (f32[1280]{0:T(1024)}, f32[1280]{0:T(1024)S(1)}, u32[]{:S(2)}) copy-start(f32[1280]{0:T(1024)S(1)} %reshape.327) | copy-start | bytes 15364
  282.4 28.5 %copy-start.14 = (f32[1280]{0:T(1024)}, f32[1280]{0:T(1024)S(1)}, u32[]{:S(2)}) copy-start(f32[1280]{0:T(1024)S(1)} %reshape.326) | copy-start | bytes 15364
  282.6 28.2 %copy-start.16 = (f32[512]{0:T(512)}, f32[512]{0:T(512)S(1)}, u32[]{:S(2)}) copy-start(f32[512]{0:T(512)S(1)} %broadcast_multiply_fusion.9) | copy-start | bytes 6148
  283.1 27.7 %copy-start.18 = (f32[512]{0:T(512)}, f32[512]{0:T(512)S(1)}, u32[]{:S(2)}) copy-start(f32[512]{0:T(512)S(1)} %add_rsqrt_fusion.1) | copy-start | bytes 6148
  641.0 302.5 %reduce-scatter.5.cloned.1.call-start = ((), (), s32[]{:S(2)}) async-start(), calls=%async_computation.8 | async-start | bytes 29491200 | tf_op jit(solution)/shard_map/reduce_scatter | solution.py:273
  702.7 533.8 %reduce-scatter.11.cloned.1.call-start = ((), (), s32[]{:S(2)}) async-start(), calls=%async_computation.11 | async-start | bytes 39321600 | tf_op jit(solution)/shard_map/reduce_scatter | solution.py:229
  718.2 811.3 %reduce-scatter.9.cloned.1.call-start = ((), (), s32[]{:S(2)}) async-start(), calls=%async_computation.10 | async-start | bytes 39321600 | tf_op jit(solution)/shard_map/reduce_scatter | solution.py:227
  733.7 824.6 %all-reduce.16.cloned.1.call-start = ((), (), s32[]{:S(2)}) async-start(), calls=%async_computation.13 | async-start | bytes 172032
  747.2 1468.0 %all-reduce.14.cloned.1.call-start = ((), (), s32[]{:S(2)}) async-start(), calls=%async_computation.12 | async-start | bytes 78643200 | tf_op jit(solution)/shard_map/psum | solution.py:278
  (22 other events, 98.3 us)
Sparse Core Ops, SparseCore 0:
  9.5 230.4 all-gather.12
  241.6 53.5 all-gather.14
  296.7 159.7 all-gather.16
  457.9 158.2 all-gather.18
  641.1 79.9 reduce-scatter.6
  723.3 220.2 reduce-scatter.4
  945.9 290.6 reduce-scatter.10
  1238.8 290.6 reduce-scatter.8
  1533.4 20.8 all-reduce.15
  1559.0 656.1 all-reduce.13
